TPU v7x, 32 devices: a whole 2x2x4 slice. The times are simulated.
32 devices in a mesh: ax: 16 (over z, x, core), az: 2 (over y).
Axes of the slice: x: 2, y: 2, z: 4, core: 2. Of those that a mesh axis runs over, the one named last changes fastest.
Arguments:
- conserved: float32 [64, 5, 32, 512], P('ax', None, None, 'az'), may hold values from -1.1 to 6.2, as said below
- cycle_modes: int32 [32], replicated, may hold values from 1 to 64, as said below
- filtered_cycles: int32 [64], P('ax'), may hold values from 1 to 32, as said below
Outputs:
- stepped: float32 [64, 5, 32, 512], P('ax', None, None, 'az')
Inputs may be any that keep to these rules, and one draw needn't show every extreme that they name: `conserved`: density is at least 0.3 and pressure at least 0.02 in every cell. `cycle_modes`: 64 and 1 both occur. `filtered_cycles`: 32 and 1 both occur.
All inputs are finite; a program needn't handle non-finite values.
Results may differ from a plain program's by a relative error of at most 0.0003.
Values sent between devices are 32-bit elements; how exact they have to be, the bound alone decides.
No kernel may reach another device: no remote copies, remote signals or barrier semaphores. Data moves between devices by JAX's collectives and lax.ppermute only.
A program may use at most 64 MiB of HBM per device.

v0:
```python
import math
import jax
import jax.numpy as jnp
from jax import lax
from jax.sharding import PartitionSpec as P

NT = 512
NRF = 32
MODE_MOST = 64
STENCIL = (0.8, -0.2, 4.0 / 105.0, -1.0 / 280.0)
GAS_FACTOR = 0.4
TIME_STEP = 0.1


def extended(cells, sides, width, closed):
    for axis, dim in sides:
        count = lax.axis_size(axis)
        ends = count if closed else count - 1
        head = lax.slice_in_dim(cells, 0, width, axis=dim)
        tail = lax.slice_in_dim(cells, cells.shape[dim] - width, cells.shape[dim], axis=dim)
        cells = jnp.concatenate(
            [
                lax.ppermute(tail, axis, [(i, (i + 1) % count) for i in range(ends)]),
                cells,
                lax.ppermute(head, axis, [((i + 1) % count, i) for i in range(ends)]),
            ],
            axis=dim,
        )
    return cells


def partner(block, axis, distance):
    count = lax.axis_size(axis)
    route = []
    for low in range(count):
        high = low | 1 << distance
        if high != low and high < count:
            route += [(low, high), (high, low)]
    return lax.ppermute(block, axis, route)


def velocities(fields):
    density = fields[:, 0]
    axial_vel = fields[:, 1] / density
    radial_vel = fields[:, 2] / density
    swirl_vel = fields[:, 3] / density
    kinetic = fields[:, 1] * axial_vel + fields[:, 2] * radial_vel + fields[:, 3] * swirl_vel
    pressure = GAS_FACTOR * (fields[:, 4] - 0.5 * kinetic)
    return (axial_vel, radial_vel, swirl_vel, pressure)


def axial_flux(fields):
    axial_vel, radial_vel, swirl_vel, pressure = velocities(fields)
    return jnp.stack(
        [
            fields[:, 1],
            fields[:, 1] * axial_vel + pressure,
            fields[:, 2] * axial_vel,
            fields[:, 3] * axial_vel,
            axial_vel * (fields[:, 4] + pressure),
        ],
        axis=1,
    )


def radial_flux(fields):
    axial_vel, radial_vel, swirl_vel, pressure = velocities(fields)
    return jnp.stack(
        [
            fields[:, 2],
            fields[:, 1] * radial_vel,
            fields[:, 2] * radial_vel + pressure,
            fields[:, 3] * radial_vel,
            radial_vel * (fields[:, 4] + pressure),
        ],
        axis=1,
    )


def swirl_flux(fields):
    axial_vel, radial_vel, swirl_vel, pressure = velocities(fields)
    return jnp.stack(
        [
            fields[:, 3],
            fields[:, 1] * swirl_vel,
            fields[:, 2] * swirl_vel,
            fields[:, 3] * swirl_vel + pressure,
            swirl_vel * (fields[:, 4] + pressure),
        ],
        axis=1,
    )


def central_difference(values, along, extent):
    result = None
    for offset, weight in zip((1, 2, 3, 4), STENCIL):
        forward_part = lax.slice_in_dim(values, 4 + offset, 4 + offset + extent, axis=along)
        backward_part = lax.slice_in_dim(values, 4 - offset, 4 - offset + extent, axis=along)
        contribution = weight * (forward_part - backward_part)
        result = contribution if result is None else result + contribution
    return result


def section_update(axial_padded, theta_padded, opposite, fields):
    stations = fields.shape[0]
    radial = fields.shape[2]
    width = fields.shape[3]
    axial_term = central_difference(axial_flux(axial_padded), 0, stations)
    flips = jnp.array([1.0, 1.0, -1.0, -1.0, 1.0], jnp.float32).reshape(1, 5, 1, 1)
    mirrored = opposite[:, :, ::-1, :] * flips
    outer_rows = jnp.broadcast_to(fields[:, :, -1:, :], (stations, 5, 4, width))
    radial_padded = jnp.concatenate([mirrored, fields, outer_rows], axis=2)
    signed_radius = (jnp.arange(radial + 8, dtype=jnp.float32) - 3.5).reshape(1, 1, -1, 1)
    radial_term = central_difference(radial_flux(radial_padded) * signed_radius, 2, radial)
    swirl_term = central_difference(swirl_flux(theta_padded), 3, width) * (NT / (2.0 * math.pi))
    axial_vel, radial_vel, swirl_vel, pressure = velocities(fields)
    nothing = jnp.zeros_like(pressure)
    source = jnp.stack(
        [nothing, nothing, fields[:, 3] * swirl_vel + pressure, -fields[:, 2] * swirl_vel, nothing],
        axis=1,
    )
    radius = (jnp.arange(radial, dtype=jnp.float32) + 0.5).reshape(1, 1, -1, 1)
    tendency = -axial_term - (radial_term + swirl_term - source) / radius
    return fields + TIME_STEP * tendency


def fourier_basis(columns):
    harmonic = jnp.arange(2 * MODE_MOST, dtype=jnp.int32) % MODE_MOST
    product = columns[:, None] * harmonic[None, :] % NT
    angle = product.astype(jnp.float32) * (2.0 * math.pi / NT)
    cosine_side = (jnp.arange(2 * MODE_MOST, dtype=jnp.int32) < MODE_MOST)[None, :]
    return jnp.where(cosine_side, jnp.cos(angle), jnp.sin(angle))


def mode_weights(cycle_modes):
    harmonic = jnp.arange(2 * MODE_MOST, dtype=jnp.int32) % MODE_MOST
    base_weight = jnp.where(harmonic == 0, 1.0 / NT, 2.0 / NT).astype(jnp.float32)
    keep = harmonic[None, :] < cycle_modes[:, None]
    return jnp.where(keep, base_weight[None, :], 0.0)


def per_device(conserved, cycle_modes, filtered_cycles):
    axial_padded = extended(conserved, (("ax", 0),), 4, False)
    theta_padded = extended(conserved, (("az", 3),), 4, True)
    position = lax.axis_index("ax")
    last_index = lax.axis_size("ax") - 1
    low_edge = jnp.broadcast_to(conserved[:1], (4,) + conserved.shape[1:])
    high_edge = jnp.broadcast_to(conserved[-1:], (4,) + conserved.shape[1:])
    axial_padded = jnp.concatenate(
        [
            jnp.where(position == 0, low_edge, axial_padded[:4]),
            axial_padded[4:-4],
            jnp.where(position == last_index, high_edge, axial_padded[-4:]),
        ],
        axis=0,
    )
    partner_bit = lax.axis_size("az").bit_length() - 2
    opposite = partner(conserved[:, :, :4, :], "az", partner_bit)
    section = section_update(axial_padded, theta_padded, opposite, conserved)
    kept_weights = mode_weights(cycle_modes)
    sector = lax.axis_index("az")
    per_sector = NRF // lax.axis_size("az")
    lines = lax.all_to_all(section, "az", split_axis=2, concat_axis=3, tiled=True)
    full_basis = fourier_basis(jnp.arange(NT, dtype=jnp.int32))
    local_weights = lax.dynamic_slice_in_dim(kept_weights, sector * per_sector, per_sector, 0)
    coefficients = jnp.einsum("afrt,tc->afrc", lines, full_basis, precision=lax.Precision.HIGHEST)
    smoothed = jnp.einsum(
        "afrc,tc->afrt",
        coefficients * local_weights[None, None],
        full_basis,
        precision=lax.Precision.HIGHEST,
    )
    local_ids = sector * per_sector + jnp.arange(per_sector, dtype=jnp.int32)
    chosen = jnp.where(
        local_ids[None, None, :, None] < filtered_cycles[:, None, None, None], smoothed, lines
    )
    result_cycles = lax.all_to_all(chosen, "az", split_axis=3, concat_axis=2, tiled=True)
    return jnp.concatenate([result_cycles, section[:, :, NRF:, :]], axis=2)


def solution(mesh):
    placed = (P("ax", None, None, "az"), P(), P("ax"))
    return jax.shard_map(
        per_device, mesh=mesh, in_specs=placed, out_specs=P("ax", None, None, "az"), check_vma=False
    )
```

profile of v0, /device:TPU:0, one launch (start us, length us, event | category | flops | bytes accessed | tf_op | source)
XLA Modules:
  0.0 92.6 jit_solution(8275054431332127691)
XLA Ops:
  0.0 1.4 %collective-permute-start.1 = (f32[4,5,32,256]{3,2,1,0:T(8,128)}, f32[4,5,32,256]{3,2,1,0:T(8,128)S(1)}, u32[]{:S(2)}, u32[]{:S(2)}) collective-permute-start(f32[4,5,32,256]{3,2,1,0:T(8,128)} %param.4), channel_id=1, source_target_pairs={{2,0},{4,2},{6,4},{8,6},{10,8},{12,10},{14,12},{16,14},{18,16},{20... | collective-permute-start | bytes 1966088 | tf_op jit(solution)/shard_map/ppermute | solution.py:25
  1.4 3.1 %collective-permute-start = (f32[4,5,32,256]{3,2,1,0:T(8,128)}, f32[4,5,32,256]{3,2,1,0:T(8,128)S(1)}, u32[]{:S(2)}, u32[]{:S(2)}) collective-permute-start(f32[4,5,32,256]{3,2,1,0:T(8,128)} %param.4), channel_id=1, source_target_pairs={{0,2},{2,4},{4,6},{6,8},{8,10},{10,12},{12,14},{14,16},{16,18},{18... | collective-permute-start | bytes 1966088 | tf_op jit(solution)/shard_map/ppermute | solution.py:23
  4.5 1.2 %fusion.67 = (f32[4,5,32,4]{3,2,1,0:T(8,128)S(1)}, f32[4,5,32,4]{3,2,1,0:T(8,128)S(1)}) fusion(f32[4,5,32,256]{3,2,1,0:T(8,128)} %param.4), kind=kLoop, calls=%fused_computation.133 | loop fusion | bytes 40960 | tf_op jit(solution)/shard_map/slice | solution.py:20
  5.7 3.1 %collective-permute-start.3 = (f32[4,5,32,4]{3,2,1,0:T(8,128)S(1)}, f32[4,5,32,4]{3,2,1,0:T(8,128)S(1)}, u32[]{:S(2)}, u32[]{:S(2)}) collective-permute-start(f32[4,5,32,4]{3,2,1,0:T(8,128)S(1)} %get-tuple-element.18), channel_id=1, source_target_pairs={{0,1},{1,0},{2,3},{3,2},{4,5},{5,4},{6,7},{7,6},{8,9},{9,8},{10,11... | collective-permute-start | bytes 30728 | tf_op jit(solution)/shard_map/ppermute | solution.py:23
  8.8 0.1 collective-permute-start.4
  8.9 1.6 %slice.194 = f32[4,5,4,256]{3,2,1,0:T(4,128)} slice(f32[4,5,32,256]{3,2,1,0:T(8,128)} %param.4), slice={[0:4], [0:5], [0:4], [0:256]} | slice | bytes 163840 | tf_op jit(solution)/shard_map/slice | solution.py:158
  10.4 1.9 %collective-permute-start.2 = (f32[4,5,4,256]{3,2,1,0:T(4,128)}, f32[4,5,4,256]{3,2,1,0:T(4,128)}, u32[]{:S(2)}, u32[]{:S(2)}) collective-permute-start(f32[4,5,4,256]{3,2,1,0:T(4,128)} %slice.194), channel_id=1, source_target_pairs={{0,1},{1,0},{2,3},{3,2},{4,5},{5,4},{6,7},{7,6},{8,9},{9,8},{10,11... | collective-permute-start | bytes 245768 | tf_op jit(solution)/shard_map/ppermute | solution.py:39
  12.4 1.0 %slice_bitcast_fusion.1 = (f32[5,32,256]{2,1,0:T(8,128)S(1)}, f32[5,32,256]{2,1,0:T(8,128)S(1)}) fusion(f32[4,5,32,256]{3,2,1,0:T(8,128)} %param.4), kind=kLoop, calls=%fused_computation.103 | loop fusion | bytes 655360 | tf_op jit(solution)/shard_map/broadcast_in_dim | solution.py:147
  13.4 0.6 iota_add_fusion.1
  14.0 0.0 copy-done
  14.0 0.1 fusion.55
  14.1 0.5 and_select_fusion
  14.6 0.0 copy-done.6
  14.6 0.6 broadcast_compare_fusion
  15.2 0.6 compare_select_fusion.1
  15.8 0.6 slice.195
  16.4 0.7 copy.42
  17.1 0.6 copy.33
  17.8 0.1 pad.3.clone
  17.8 1.3 %dynamic-slice = s32[16]{0:T(128)} dynamic-slice(s32[32]{0:T(128)} %param.5, s32[]{:T(128)S(6)} %select_n.78), dynamic_slice_sizes={16} | dynamic-slice | bytes 132 | tf_op jit(solution)/shard_map/dynamic_slice | solution.py:165
  19.1 0.0 collective-permute-done.3
  19.1 4.8 %collective-permute-done.4 = f32[4,5,32,4]{3,2,1,0:T(8,128)} collective-permute-done((f32[4,5,32,4]{3,2,1,0:T(8,128)S(1)}, f32[4,5,32,4]{3,2,1,0:T(8,128)}, u32[]{:S(2)}, u32[]{:S(2)}) %collective-permute-start.4) | collective-permute-done | bytes 10272 | tf_op jit(solution)/shard_map/ppermute | solution.py:25
  23.9 1.4 %pad_maximum_fusion.1 = f32[4,5,32,264]{3,2,1,0:T(8,128)S(1)} fusion(f32[4,5,32,4]{3,2,1,0:T(8,128)} %collective-permute-done.4, f32[4,5,32,256]{3,2,1,0:T(8,128)S(1)} %copy-done, f32[4,5,32,4]{3,2,1,0:T(8,128)S(1)} %collective-permute-done.3), kind=kLoop, calls=%fused_computation.3 | loop fusion | flops 337920 | bytes 1351680 | tf_op jit(solution)/shard_map/concatenate | solution.py:21
  25.3 0.0 copy-start.1
  25.4 0.1 add_dynamic-update-slice_fusion.1
  25.5 0.1 collective-permute-done.2
  25.7 1.5 %rev.3 = f32[4,5,4,256]{3,2,1,0:T(4,128)} reverse(f32[4,5,4,256]{3,2,1,0:T(4,128)} %collective-permute-done.2), dimensions={2} | reverse | bytes 163840 | tf_op jit(solution)/shard_map/rev | solution.py:110
  27.2 0.0 copy-done.1
  27.2 1.0 %broadcast_multiply_fusion.1 = f32[4,5,4,256]{3,2,1,0:T(4,128)S(1)} fusion(f32[4,5,4,256]{3,2,1,0:T(4,128)} %rev.3, f32[5]{0:T(128)S(1)} %copy-done.1), kind=kLoop, calls=%fused_computation.115 | loop fusion | flops 20480 | bytes 163860 | tf_op jit(solution)/shard_map/mul | solution.py:110
  28.1 0.8 broadcast_in_dim.74
  28.9 0.1 pad_maximum_fusion.2
  29.0 0.0 copy-start.2
  29.1 0.1 add_dynamic-update-slice_fusion.2
  29.3 0.4 copy-done.2
  29.7 0.1 broadcast_multiply_fusion
  29.8 0.0 collective-permute-done.1
  29.8 0.1 broadcast_select_fusion
  29.9 0.0 collective-permute-done
  29.9 0.1 broadcast_select_fusion.1
  30.0 0.2 pad_maximum_fusion
  30.3 0.2 add_dynamic-update-slice_fusion
  30.5 0.1 multiply_dynamic-update-slice_fusion.2
  30.5 0.1 multiply_dynamic-update-slice_fusion.1
  30.6 0.1 multiply_dynamic-update-slice_fusion
  30.7 1.5 %multiply_add_fusion = f32[4,5,32,256]{3,2,1,0:T(8,128)S(1)} fusion(f32[4,5,32,256]{3,2,1,0:T(8,128)S(1)} %copy-done, f32[4,1,32,256]{3,2,1,0:T(8,128)S(1)} %get-tuple-element.21, f32[4,1,32,256]{3,2,1,0:T(8,128)S(1)} %get-tuple-element.20, f32[4,5,32,264]{3,2,1,0:T(8,128)S(1)} %multiply_dynamic-update-slice_fusion.3, ...), kind=kLoop, calls=%fused_computation.45 | loop fusion | flops 7208960 | bytes 17301672 | tf_op jit(solution)/shard_map/add | solution.py:124
  32.3 0.0 copy-start.3
  32.3 0.0 copy-start.4
  32.3 0.0 copy-start.5
  32.3 1.4 %copy.34 = f32[4,5,32,256]{3,1,0,2:T(8,128)} copy(f32[4,5,32,256]{3,2,1,0:T(8,128)S(1)} %multiply_add_fusion) | data formatting | bytes 1310720 | tf_op jit(solution)/shard_map/add | solution.py:124
  33.7 3.7 %all-to-all-start = ((f32[4,5,32,256]{3,1,0,2:T(8,128)}), f32[4,5,32,256]{3,1,0,2:T(8,128)S(1)}, u32[]{:S(2)}, u32[]{:S(2)}) async-start(f32[4,5,32,256]{3,1,0,2:T(8,128)} %copy.34), calls=%async_computation | async-start | bytes 2097152 | tf_op jit(solution)/shard_map/all_to_all | solution.py:163
  37.4 0.0 copy-done.4
  37.5 0.1 compare_select_fusion
  37.5 15.0 %all-to-all-done = f32[4,5,32,256]{3,1,0,2:T(8,128)S(1)} async-done(((f32[4,5,32,256]{3,1,0,2:T(8,128)}), f32[4,5,32,256]{3,1,0,2:T(8,128)S(1)}, u32[]{:S(2)}, u32[]{:S(2)}) %all-to-all-start) | async-done | bytes 655392 | tf_op jit(solution)/shard_map/all_to_all | solution.py:163
  52.5 0.5 copy.41
  53.0 0.5 all_to_all.29
  53.5 1.7 %convolution_multiply_fusion = f32[4,5,16,128]{3,2,1,0:T(8,128)S(1)} fusion(f32[4,5,16,512]{3,2,1,0:T(8,128)S(1)} %all_to_all.29, s32[128]{0:T(128)S(1)} %copy-done.3, pred[128]{0:T(512)(128)(4,1)S(1)} %iota_compare_fusion, f32[16,128]{1,0:T(8,128)S(1)} %compare_select_fusion), kind=kOutput, calls=%fused_computation.2 | convolution fusion | flops 252682240 | bytes 828032 | tf_op jit(solution)/shard_map/afrt,tc->afrc/dot_general | solution.py:166
  55.3 1.7 %convolution_select_fusion = f32[4,5,16,512]{3,2,1,0:T(8,128)S(1)} fusion(f32[4,5,16,512]{3,2,1,0:T(8,128)S(1)} %all_to_all.29, f32[4,5,16,128]{3,2,1,0:T(8,128)S(1)} %convolution_multiply_fusion, pred[4,16]{1,0:T(4,128)(4,1)S(1)} %copy-done.7, s32[128]{0:T(128)S(1)} %copy-done.3, pred[128]{0:T(512)(128)(4,1)S(1)} %iota_compare_fusion), kind=kOutput, calls=%fused_computation.1 | convolution fusion | flops 252805120 | bytes 1475264 | tf_op jit(solution)/shard_map/afrc,tc->afrt/dot_general | solution.py:167
  57.0 3.5 %copy.36 = f32[4,5,16,512]{2,0,1,3:T(4,128)} copy(f32[4,5,16,512]{3,2,1,0:T(8,128)S(1)} %convolution_select_fusion) | data formatting | bytes 1310720 | tf_op jit(solution)/shard_map/jit(_where)/select_n | solution.py:174
  60.5 5.7 %reshape.69 = f32[2,1,81920]{2,1,0:T(1,128)S(1)} reshape(f32[512,5,4,16]{3,2,1,0:T(4,128)} %bitcast.27) | data formatting | bytes 1310720
  66.2 12.1 %all_to_all.36 = f32[2,1,81920]{2,1,0:T(1,128)S(1)} all-to-all(f32[2,1,81920]{2,1,0:T(1,128)S(1)} %reshape.69), channel_id=1, replica_groups=mesh['ax'=16,'az'=2] {'az'}, dimensions={0} | all-to-all | bytes 1310720 | tf_op jit(solution)/shard_map/all_to_all | solution.py:177
  78.3 0.5 broadcast.144
  78.8 2.7 %reduce = f32[2,81920]{1,0:T(2,128)S(1)} reduce(f32[2,1,81920]{2,1,0:T(1,128)S(1)} %all_to_all.36, f32[]{:T(128)} %broadcast.144), dimensions={1}, to_apply=%all_to_all.30.reduce_sub_computation | reduce | bytes 1310724 | tf_op jit(solution)/shard_map/all_to_all | solution.py:177
  81.5 6.3 %reshape.70 = f32[512,5,4,16]{3,2,1,0:T(4,128)} reshape(f32[2,81920]{1,0:T(2,128)S(1)} %reduce) | data formatting | bytes 1310720
  87.8 4.8 %copy.37 = f32[4,5,2,16,256]{4,3,2,1,0:T(8,128)} copy(f32[4,5,2,16,256]{3,0,1,4,2:T(4,128)} %bitcast.28) | data formatting | bytes 1310720 | tf_op jit(solution)/shard_map/all_to_all | solution.py:177
  (20 shorter events, 0.3 us)
Async XLA Ops:
  0.0 14.0 %copy-start = (f32[4,5,32,256]{3,2,1,0:T(8,128)S(1)}, f32[4,5,32,256]{3,2,1,0:T(8,128)}, u32[]{:S(2)}) copy-start(f32[4,5,32,256]{3,2,1,0:T(8,128)} %param.4) | copy-start | bytes 1966084
  0.0 14.6 %copy-start.6 = (s32[4]{0:T(128)S(1)}, s32[4]{0:T(128)}, u32[]{:S(2)}) copy-start(s32[4]{0:T(128)} %param.6) | copy-start | bytes 52
  0.0 29.8 %collective-permute-start.1 = (f32[4,5,32,256]{3,2,1,0:T(8,128)}, f32[4,5,32,256]{3,2,1,0:T(8,128)S(1)}, u32[]{:S(2)}, u32[]{:S(2)}) collective-permute-start(f32[4,5,32,256]{3,2,1,0:T(8,128)} %param.4), channel_id=1, source_target_pairs={{2,0},{4,2},{6,4},{8,6},{10,8},{12,10},{14,12},{16,14},{18,16},{20... | collective-permute-start | bytes 1966088 | tf_op jit(solution)/shard_map/ppermute | solution.py:25
  1.4 28.5 %collective-permute-start = (f32[4,5,32,256]{3,2,1,0:T(8,128)}, f32[4,5,32,256]{3,2,1,0:T(8,128)S(1)}, u32[]{:S(2)}, u32[]{:S(2)}) collective-permute-start(f32[4,5,32,256]{3,2,1,0:T(8,128)} %param.4), channel_id=1, source_target_pairs={{0,2},{2,4},{4,6},{6,8},{8,10},{10,12},{12,14},{14,16},{16,18},{18... | collective-permute-start | bytes 1966088 | tf_op jit(solution)/shard_map/ppermute | solution.py:23
  5.7 13.4 %collective-permute-start.3 = (f32[4,5,32,4]{3,2,1,0:T(8,128)S(1)}, f32[4,5,32,4]{3,2,1,0:T(8,128)S(1)}, u32[]{:S(2)}, u32[]{:S(2)}) collective-permute-start(f32[4,5,32,4]{3,2,1,0:T(8,128)S(1)} %get-tuple-element.18), channel_id=1, source_target_pairs={{0,1},{1,0},{2,3},{3,2},{4,5},{5,4},{6,7},{7,6},{8,9},{9,8},{10,11... | collective-permute-start | bytes 30728 | tf_op jit(solution)/shard_map/ppermute | solution.py:23
  8.8 15.1 %collective-permute-start.4 = (f32[4,5,32,4]{3,2,1,0:T(8,128)S(1)}, f32[4,5,32,4]{3,2,1,0:T(8,128)}, u32[]{:S(2)}, u32[]{:S(2)}) collective-permute-start(f32[4,5,32,4]{3,2,1,0:T(8,128)S(1)} %get-tuple-element.19), channel_id=1, source_target_pairs={{1,0},{0,1},{3,2},{2,3},{5,4},{4,5},{7,6},{6,7},{9,8},{8,9},{11,10... | collective-permute-start | bytes 30728 | tf_op jit(solution)/shard_map/ppermute | solution.py:25
  10.4 15.2 %collective-permute-start.2 = (f32[4,5,4,256]{3,2,1,0:T(4,128)}, f32[4,5,4,256]{3,2,1,0:T(4,128)}, u32[]{:S(2)}, u32[]{:S(2)}) collective-permute-start(f32[4,5,4,256]{3,2,1,0:T(4,128)} %slice.194), channel_id=1, source_target_pairs={{0,1},{1,0},{2,3},{3,2},{4,5},{5,4},{6,7},{7,6},{8,9},{9,8},{10,11... | collective-permute-start | bytes 245768 | tf_op jit(solution)/shard_map/ppermute | solution.py:39
  25.3 1.9 %copy-start.1 = (f32[5]{0:T(128)S(1)}, f32[5]{0:T(128)}, u32[]{:S(2)}) copy-start(f32[5]{0:T(128)} %constant.88.clone) | copy-start | bytes 64
  29.0 0.7 copy-start.2
  32.3 5.2 %copy-start.3 = (s32[128]{0:T(128)S(1)}, s32[128]{0:T(128)}, u32[]{:S(2)}) copy-start(s32[128]{0:T(128)} %and_select_fusion) | copy-start | bytes 1540
  32.3 5.2 %copy-start.4 = (f32[128]{0:T(128)S(1)}, f32[128]{0:T(128)}, u32[]{:S(2)}) copy-start(f32[128]{0:T(128)} %compare_select_fusion.1) | copy-start | bytes 1540
  32.3 5.2 %copy-start.5 = (s32[16]{0:T(128)S(1)}, s32[16]{0:T(128)}, u32[]{:S(2)}) copy-start(s32[16]{0:T(128)} %dynamic-slice) | copy-start | bytes 196
  33.7 18.8 %all-to-all-start = ((f32[4,5,32,256]{3,1,0,2:T(8,128)}), f32[4,5,32,256]{3,1,0,2:T(8,128)S(1)}, u32[]{:S(2)}, u32[]{:S(2)}) async-start(f32[4,5,32,256]{3,1,0,2:T(8,128)} %copy.34), calls=%async_computation | async-start | bytes 2097152 | tf_op jit(solution)/shard_map/all_to_all | solution.py:163
  52.5 2.8 %copy-start.7 = (pred[4,16]{1,0:T(4,128)(4,1)S(1)}, pred[4,16]{1,0:T(4,128)(4,1)}, u32[]{:S(2)}) copy-start(pred[4,16]{1,0:T(4,128)(4,1)} %broadcast_compare_fusion) | copy-start | bytes 196
where the time goes:
time: 93.3 us; the launch traced here: 92.6 us
  local copies, waits for them, and re-layouts  33.1 us (35%)
  waiting for transfers between devices  19.9 us (21%)
  starting transfers between devices  13.3 us (14%)
  blocking collectives  12.1 us (13%)
  other arithmetic  10.5 us (11%)
  matrix products  3.43 us (4%)
    all_to_all x1, waiting for transfers between devices, per_device(): lax.all_to_all(section, 'az', split_axis=2, concat_axis=3, tiled=True)  15 us
    unnamed x21, local copies, waits for them, and re-layouts  12.5 us
    all_to_all x1, blocking collectives, per_device(): lax.all_to_all(chosen, 'az', split_axis=3, concat_axis=2, tiled=True)  12.1 us
    ppermute x2, starting transfers between devices, extended(): lax.ppermute(tail, axis, [(i, (i + 1) % count) for i in range(ends)])  6.14 us
    all_to_all x2, local copies, waits for them, and re-layouts, per_device(): lax.all_to_all(chosen, 'az', split_axis=3, concat_axis=2, tiled=True)  5.32 us
    ppermute x2, waiting for transfers between devices, extended(): lax.ppermute(head, axis, [((i + 1) % count, i) for i in range(ends)])  4.79 us
    all_to_all x1, starting transfers between devices, per_device(): lax.all_to_all(section, 'az', split_axis=2, concat_axis=3, tiled=True)  3.75 us
    select_n x1, local copies, waits for them, and re-layouts, per_device(): jnp.where(local_ids[None, None, :, None] < filtered_cycles[:, None, None,...  3.52 us
  transfers between devices with their start and end apart: 6, of which 3 were waited for; matrix products, arithmetic and copies ran while one was open for 16% of the time, Pallas kernels for 0%

commit v1 on v0

--- a/solution.py
+++ b/solution.py
@@ -174,7 +174,10 @@
     chosen = jnp.where(
         local_ids[None, None, :, None] < filtered_cycles[:, None, None, None], smoothed, lines
     )
-    result_cycles = lax.all_to_all(chosen, "az", split_axis=3, concat_axis=2, tiled=True)
+    result_cycles = jnp.concatenate(
+        lax.all_to_all(jnp.stack(jnp.split(chosen, lax.axis_size("az"), axis=3)), "az", 0, 0),
+        axis=2,
+    )
     return jnp.concatenate([result_cycles, section[:, :, NRF:, :]], axis=2)
 
 

time: 93.3 us -> 70.7 us (0.76)
  local copies, waits for them, and re-layouts: 33.1 us -> 12.6 us
  other arithmetic: 10.5 us -> 7.8 us
    unnamed x21, local copies, waits for them, and re-layouts: 12.5 us -> 0.48 us
    all_to_all x2 -> x0, local copies, waits for them, and re-layouts: 5.32 us -> none  [per_device(): lax.all_to_all(chosen, 'az', split_axis=3, concat_axis=2, tiled=True)]
    select_n x1 -> x0, local copies, waits for them, and re-layouts: 3.52 us -> none  [per_device(): jnp.where(local_ids[None, None, :, None] < filtered_cycles[:, None, None,...]
    all_to_all x1 -> x0, other arithmetic: 2.7 us -> none  [per_device(): lax.all_to_all(chosen, 'az', split_axis=3, concat_axis=2, tiled=True)]
  transfers between devices with their start and end apart: 6 -> 6, of which waited for: 3 -> 3; matrix products, arithmetic and copies ran while one was open for 16% -> 20% of each run, Pallas kernels for 0% -> 0%
where the time goes in v1:
time: 70.7 us; the launch traced here: 70.1 us
  waiting for transfers between devices  20.5 us (29%)
  starting transfers between devices  13.3 us (19%)
  local copies, waits for them, and re-layouts  12.6 us (18%)
  blocking collectives  12.1 us (17%)
  other arithmetic  7.8 us (11%)
  matrix products  3.43 us (5%)
    all_to_all x1, waiting for transfers between devices, per_device(): lax.all_to_all(section, 'az', split_axis=2, concat_axis=3, tiled=True)  15 us
    all_to_all x1, blocking collectives, per_device(): lax.all_to_all(jnp.stack(jnp.split(chosen, lax.axis_size('az'), axis=3)),...  12.1 us
    ppermute x2, starting transfers between devices, extended(): lax.ppermute(tail, axis, [(i, (i + 1) % count) for i in range(ends)])  6.15 us
    ppermute x2, waiting for transfers between devices, extended(): lax.ppermute(head, axis, [((i + 1) % count, i) for i in range(ends)])  5.4 us
    all_to_all x1, starting transfers between devices, per_device(): lax.all_to_all(section, 'az', split_axis=2, concat_axis=3, tiled=True)  3.75 us
    ppermute x1, starting transfers between devices, partner(): return lax.ppermute(block, axis, route)  1.95 us
    dot_general x1, matrix products, per_device(): jnp.einsum('afrt,tc->afrc', lines, full_basis, precision=lax.Precision.HI...  1.72 us
    dot_general x1, matrix products, per_device(): jnp.einsum('afrc,tc->afrt', coefficients * local_weights[None, None], ful...  1.72 us
  transfers between devices with their start and end apart: 6, of which 3 were waited for; matrix products, arithmetic and copies ran while one was open for 20% of the time, Pallas kernels for 0%

profile of v1, /device:TPU:0, one launch (start us, length us, event | category | flops | bytes accessed | tf_op | source)
XLA Modules:
  0.0 70.1 jit_solution(7643926990583324465)
XLA Ops:
  0.0 1.4 %collective-permute-start.1 = (f32[4,5,32,256]{3,2,1,0:T(8,128)}, f32[4,5,32,256]{3,2,1,0:T(8,128)S(1)}, u32[]{:S(2)}, u32[]{:S(2)}) collective-permute-start(f32[4,5,32,256]{3,2,1,0:T(8,128)} %param.4), channel_id=1, source_target_pairs={{2,0},{4,2},{6,4},{8,6},{10,8},{12,10},{14,12},{16,14},{18,16},{20... | collective-permute-start | bytes 1966088 | tf_op jit(solution)/shard_map/ppermute | solution.py:25
  1.4 3.1 %collective-permute-start = (f32[4,5,32,256]{3,2,1,0:T(8,128)}, f32[4,5,32,256]{3,2,1,0:T(8,128)S(1)}, u32[]{:S(2)}, u32[]{:S(2)}) collective-permute-start(f32[4,5,32,256]{3,2,1,0:T(8,128)} %param.4), channel_id=1, source_target_pairs={{0,2},{2,4},{4,6},{6,8},{8,10},{10,12},{12,14},{14,16},{16,18},{18... | collective-permute-start | bytes 1966088 | tf_op jit(solution)/shard_map/ppermute | solution.py:23
  4.5 1.2 %fusion.67 = (f32[4,5,32,4]{3,2,1,0:T(8,128)S(1)}, f32[4,5,32,4]{3,2,1,0:T(8,128)S(1)}) fusion(f32[4,5,32,256]{3,2,1,0:T(8,128)} %param.4), kind=kLoop, calls=%fused_computation.136 | loop fusion | bytes 40960 | tf_op jit(solution)/shard_map/slice | solution.py:20
  5.7 3.1 %collective-permute-start.3 = (f32[4,5,32,4]{3,2,1,0:T(8,128)S(1)}, f32[4,5,32,4]{3,2,1,0:T(8,128)S(1)}, u32[]{:S(2)}, u32[]{:S(2)}) collective-permute-start(f32[4,5,32,4]{3,2,1,0:T(8,128)S(1)} %get-tuple-element.20), channel_id=1, source_target_pairs={{0,1},{1,0},{2,3},{3,2},{4,5},{5,4},{6,7},{7,6},{8,9},{9,8},{10,11... | collective-permute-start | bytes 30728 | tf_op jit(solution)/shard_map/ppermute | solution.py:23
  8.8 0.1 collective-permute-start.4
  8.9 1.6 %slice.194 = f32[4,5,4,256]{3,2,1,0:T(4,128)} slice(f32[4,5,32,256]{3,2,1,0:T(8,128)} %param.4), slice={[0:4], [0:5], [0:4], [0:256]} | slice | bytes 163840 | tf_op jit(solution)/shard_map/slice | solution.py:158
  10.5 1.9 %collective-permute-start.2 = (f32[4,5,4,256]{3,2,1,0:T(4,128)}, f32[4,5,4,256]{3,2,1,0:T(4,128)}, u32[]{:S(2)}, u32[]{:S(2)}) collective-permute-start(f32[4,5,4,256]{3,2,1,0:T(4,128)} %slice.194), channel_id=1, source_target_pairs={{0,1},{1,0},{2,3},{3,2},{4,5},{5,4},{6,7},{7,6},{8,9},{9,8},{10,11... | collective-permute-start | bytes 245768 | tf_op jit(solution)/shard_map/ppermute | solution.py:39
  12.4 1.0 %slice_bitcast_fusion.3 = (f32[5,32,256]{2,1,0:T(8,128)S(1)}, f32[5,32,256]{2,1,0:T(8,128)S(1)}) fusion(f32[4,5,32,256]{3,2,1,0:T(8,128)} %param.4), kind=kLoop, calls=%fused_computation.106 | loop fusion | bytes 655360 | tf_op jit(solution)/shard_map/broadcast_in_dim | solution.py:147
  13.4 0.5 iota_add_fusion.1
  14.0 0.0 copy-done
  14.0 0.1 fusion.55
  14.1 0.5 and_select_fusion
  14.6 0.0 copy-done.6
  14.6 0.6 broadcast_compare_fusion
  15.2 0.6 compare_select_fusion.1
  15.8 0.6 slice.195
  16.4 0.7 %copy.39 = f32[4,5,1,256]{3,0,1,2:T(4,128)S(1)} copy(f32[4,5,1,256]{3,2,1,0:T(1,128)} %slice.195) | data formatting | bytes 40960 | tf_op jit(solution)/shard_map/slice | solution.py:111
  17.2 0.6 copy.31
  17.8 0.1 pad.5.clone
  17.9 0.0 copy-done.7
  17.9 0.6 dynamic-slice
  18.5 0.0 collective-permute-done.3
  18.5 5.4 %collective-permute-done.4 = f32[4,5,32,4]{3,2,1,0:T(8,128)} collective-permute-done((f32[4,5,32,4]{3,2,1,0:T(8,128)S(1)}, f32[4,5,32,4]{3,2,1,0:T(8,128)}, u32[]{:S(2)}, u32[]{:S(2)}) %collective-permute-start.4) | collective-permute-done | bytes 10272 | tf_op jit(solution)/shard_map/ppermute | solution.py:25
  23.9 1.4 %pad_maximum_fusion.1 = f32[4,5,32,264]{3,2,1,0:T(8,128)S(1)} fusion(f32[4,5,32,4]{3,2,1,0:T(8,128)} %collective-permute-done.4, f32[4,5,32,256]{3,2,1,0:T(8,128)S(1)} %copy-done, f32[4,5,32,4]{3,2,1,0:T(8,128)S(1)} %collective-permute-done.3), kind=kLoop, calls=%fused_computation.3 | loop fusion | flops 337920 | bytes 1351680 | tf_op jit(solution)/shard_map/concatenate | solution.py:21
  25.3 0.0 copy-start.1
  25.4 0.1 add_dynamic-update-slice_fusion.1
  25.5 0.1 collective-permute-done.2
  25.7 1.5 %rev.3 = f32[4,5,4,256]{3,2,1,0:T(4,128)} reverse(f32[4,5,4,256]{3,2,1,0:T(4,128)} %collective-permute-done.2), dimensions={2} | reverse | bytes 163840 | tf_op jit(solution)/shard_map/rev | solution.py:110
  27.2 0.0 copy-done.1
  27.2 1.0 %broadcast_multiply_fusion.1 = f32[4,5,4,256]{3,2,1,0:T(4,128)S(1)} fusion(f32[4,5,4,256]{3,2,1,0:T(4,128)} %rev.3, f32[5]{0:T(128)S(1)} %copy-done.1), kind=kLoop, calls=%fused_computation.118 | loop fusion | flops 20480 | bytes 163860 | tf_op jit(solution)/shard_map/mul | solution.py:110
  28.2 0.8 %broadcast_in_dim.74 = f32[4,5,4,256]{3,2,1,0:T(4,128)S(1)} broadcast(f32[4,5,256]{2,1,0:T(8,128)} %copy.31), dimensions={0,1,3} | broadcast | bytes 102400 | tf_op jit(solution)/shard_map/broadcast_in_dim | solution.py:111
  28.9 0.1 pad_maximum_fusion.2
  29.0 0.0 copy-start.2
  29.1 0.1 add_dynamic-update-slice_fusion.2
  29.3 0.4 copy-done.2
  29.7 0.1 broadcast_multiply_fusion
  29.8 0.0 collective-permute-done.1
  29.8 0.1 broadcast_select_fusion
  29.9 0.0 collective-permute-done
  29.9 0.1 broadcast_select_fusion.1
  30.0 0.2 pad_maximum_fusion
  30.2 0.2 add_dynamic-update-slice_fusion
  30.4 0.1 multiply_dynamic-update-slice_fusion.2
  30.5 0.1 multiply_dynamic-update-slice_fusion.1
  30.6 0.1 multiply_dynamic-update-slice_fusion
  30.7 1.5 %multiply_add_fusion = f32[4,5,32,256]{3,2,1,0:T(8,128)S(1)} fusion(f32[4,5,32,256]{3,2,1,0:T(8,128)S(1)} %copy-done, f32[4,1,32,256]{3,2,1,0:T(8,128)S(1)} %get-tuple-element.23, f32[4,1,32,256]{3,2,1,0:T(8,128)S(1)} %get-tuple-element.22, f32[4,5,32,264]{3,2,1,0:T(8,128)S(1)} %multiply_dynamic-update-slice_fusion.3, ...), kind=kLoop, calls=%fused_computation.46 | loop fusion | flops 7208960 | bytes 17301672 | tf_op jit(solution)/shard_map/add | solution.py:124
  32.2 0.0 copy-start.3
  32.2 0.0 copy-start.4
  32.2 0.0 copy-start.5
  32.2 1.4 %copy.32 = f32[4,5,32,256]{3,1,0,2:T(8,128)} copy(f32[4,5,32,256]{3,2,1,0:T(8,128)S(1)} %multiply_add_fusion) | data formatting | bytes 1310720 | tf_op jit(solution)/shard_map/add | solution.py:124
  33.6 3.7 %all-to-all-start = ((f32[4,5,32,256]{3,1,0,2:T(8,128)}), f32[4,5,32,256]{3,1,0,2:T(8,128)S(1)}, u32[]{:S(2)}, u32[]{:S(2)}) async-start(f32[4,5,32,256]{3,1,0,2:T(8,128)} %copy.32), calls=%async_computation | async-start | bytes 2097152 | tf_op jit(solution)/shard_map/all_to_all | solution.py:163
  37.4 0.0 copy-done.3
  37.4 0.0 copy-done.4
  37.4 0.0 copy-done.5
  37.4 0.1 compare_select_fusion
  37.5 15.0 %all-to-all-done = f32[4,5,32,256]{3,1,0,2:T(8,128)S(1)} async-done(((f32[4,5,32,256]{3,1,0,2:T(8,128)}), f32[4,5,32,256]{3,1,0,2:T(8,128)S(1)}, u32[]{:S(2)}, u32[]{:S(2)}) %all-to-all-start) | async-done | bytes 655392 | tf_op jit(solution)/shard_map/all_to_all | solution.py:163
  52.4 0.5 copy.38
  53.0 0.5 all_to_all.19
  53.5 1.7 %convolution_multiply_fusion = f32[4,5,16,128]{3,2,1,0:T(8,128)S(1)} fusion(f32[4,5,16,512]{3,2,1,0:T(8,128)S(1)} %all_to_all.19, s32[128]{0:T(128)S(1)} %copy-done.3, pred[128]{0:T(512)(128)(4,1)S(1)} %iota_compare_fusion, f32[16,128]{1,0:T(8,128)S(1)} %compare_select_fusion), kind=kOutput, calls=%fused_computation.2 | convolution fusion | flops 252682240 | bytes 828032 | tf_op jit(solution)/shard_map/afrt,tc->afrc/dot_general | solution.py:166
  55.2 1.7 %convolution_select_fusion = f32[4,5,16,512]{3,2,1,0:T(8,128)S(1)} fusion(f32[4,5,16,512]{3,2,1,0:T(8,128)S(1)} %all_to_all.19, f32[4,5,16,128]{3,2,1,0:T(8,128)S(1)} %convolution_multiply_fusion, pred[4,16]{1,0:T(4,128)(4,1)S(1)} %copy-done.8, s32[128]{0:T(128)S(1)} %copy-done.3, pred[128]{0:T(512)(128)(4,1)S(1)} %iota_compare_fusion), kind=kOutput, calls=%fused_computation.1 | convolution fusion | flops 252805120 | bytes 1475264 | tf_op jit(solution)/shard_map/afrc,tc->afrt/dot_general | solution.py:167
  56.9 0.1 slice_bitcast_fusion.1
  57.0 0.1 pad_maximum_fusion.3
  57.1 12.1 %all_to_all.23 = f32[2,4,5,16,256]{4,3,2,1,0:T(8,128)S(1)} all-to-all(f32[2,4,5,16,256]{4,3,2,1,0:T(8,128)S(1)} %pad_maximum_fusion.3), channel_id=1, replica_groups=mesh['ax'=16,'az'=2] {'az'}, dimensions={0} | all-to-all | bytes 1310720 | tf_op jit(solution)/shard_map/all_to_all | solution.py:178
  69.2 0.9 %copy.34 = f32[4,5,2,16,256]{4,3,2,1,0:T(8,128)} copy(f32[4,5,2,16,256]{4,3,1,0,2:T(8,128)S(1)} %bitcast.29) | data formatting | bytes 1310720 | tf_op jit(solution)/shard_map/reshape | solution.py:177
  (19 shorter events, 0.3 us)
Async XLA Ops:
  0.0 14.0 %copy-start = (f32[4,5,32,256]{3,2,1,0:T(8,128)S(1)}, f32[4,5,32,256]{3,2,1,0:T(8,128)}, u32[]{:S(2)}) copy-start(f32[4,5,32,256]{3,2,1,0:T(8,128)} %param.4) | copy-start | bytes 1966084
  0.0 14.6 %copy-start.6 = (s32[4]{0:T(128)S(1)}, s32[4]{0:T(128)}, u32[]{:S(2)}) copy-start(s32[4]{0:T(128)} %param.6) | copy-start | bytes 52
  0.0 17.8 %copy-start.7 = (s32[32]{0:T(128)S(1)}, s32[32]{0:T(128)}, u32[]{:S(2)}) copy-start(s32[32]{0:T(128)} %param.5) | copy-start | bytes 388
  0.0 29.8 %collective-permute-start.1 = (f32[4,5,32,256]{3,2,1,0:T(8,128)}, f32[4,5,32,256]{3,2,1,0:T(8,128)S(1)}, u32[]{:S(2)}, u32[]{:S(2)}) collective-permute-start(f32[4,5,32,256]{3,2,1,0:T(8,128)} %param.4), channel_id=1, source_target_pairs={{2,0},{4,2},{6,4},{8,6},{10,8},{12,10},{14,12},{16,14},{18,16},{20... | collective-permute-start | bytes 1966088 | tf_op jit(solution)/shard_map/ppermute | solution.py:25
  1.4 28.5 %collective-permute-start = (f32[4,5,32,256]{3,2,1,0:T(8,128)}, f32[4,5,32,256]{3,2,1,0:T(8,128)S(1)}, u32[]{:S(2)}, u32[]{:S(2)}) collective-permute-start(f32[4,5,32,256]{3,2,1,0:T(8,128)} %param.4), channel_id=1, source_target_pairs={{0,2},{2,4},{4,6},{6,8},{8,10},{10,12},{12,14},{14,16},{16,18},{18... | collective-permute-start | bytes 1966088 | tf_op jit(solution)/shard_map/ppermute | solution.py:23
  5.7 12.8 %collective-permute-start.3 = (f32[4,5,32,4]{3,2,1,0:T(8,128)S(1)}, f32[4,5,32,4]{3,2,1,0:T(8,128)S(1)}, u32[]{:S(2)}, u32[]{:S(2)}) collective-permute-start(f32[4,5,32,4]{3,2,1,0:T(8,128)S(1)} %get-tuple-element.20), channel_id=1, source_target_pairs={{0,1},{1,0},{2,3},{3,2},{4,5},{5,4},{6,7},{7,6},{8,9},{9,8},{10,11... | collective-permute-start | bytes 30728 | tf_op jit(solution)/shard_map/ppermute | solution.py:23
  8.8 15.1 %collective-permute-start.4 = (f32[4,5,32,4]{3,2,1,0:T(8,128)S(1)}, f32[4,5,32,4]{3,2,1,0:T(8,128)}, u32[]{:S(2)}, u32[]{:S(2)}) collective-permute-start(f32[4,5,32,4]{3,2,1,0:T(8,128)S(1)} %get-tuple-element.21), channel_id=1, source_target_pairs={{1,0},{0,1},{3,2},{2,3},{5,4},{4,5},{7,6},{6,7},{9,8},{8,9},{11,10... | collective-permute-start | bytes 30728 | tf_op jit(solution)/shard_map/ppermute | solution.py:25
  10.5 15.2 %collective-permute-start.2 = (f32[4,5,4,256]{3,2,1,0:T(4,128)}, f32[4,5,4,256]{3,2,1,0:T(4,128)}, u32[]{:S(2)}, u32[]{:S(2)}) collective-permute-start(f32[4,5,4,256]{3,2,1,0:T(4,128)} %slice.194), channel_id=1, source_target_pairs={{0,1},{1,0},{2,3},{3,2},{4,5},{5,4},{6,7},{7,6},{8,9},{9,8},{10,11... | collective-permute-start | bytes 245768 | tf_op jit(solution)/shard_map/ppermute | solution.py:39
  25.3 1.9 %copy-start.1 = (f32[5]{0:T(128)S(1)}, f32[5]{0:T(128)}, u32[]{:S(2)}) copy-start(f32[5]{0:T(128)} %constant.88.clone) | copy-start | bytes 64
  29.0 0.6 copy-start.2
  32.2 5.2 %copy-start.3 = (s32[128]{0:T(128)S(1)}, s32[128]{0:T(128)}, u32[]{:S(2)}) copy-start(s32[128]{0:T(128)} %and_select_fusion) | copy-start | bytes 1540
  32.2 5.2 %copy-start.4 = (f32[128]{0:T(128)S(1)}, f32[128]{0:T(128)}, u32[]{:S(2)}) copy-start(f32[128]{0:T(128)} %compare_select_fusion.1) | copy-start | bytes 1540
  32.2 5.2 %copy-start.5 = (s32[16]{0:T(128)S(1)}, s32[16]{0:T(128)}, u32[]{:S(2)}) copy-start(s32[16]{0:T(128)} %dynamic-slice) | copy-start | bytes 196
  33.6 18.8 %all-to-all-start = ((f32[4,5,32,256]{3,1,0,2:T(8,128)}), f32[4,5,32,256]{3,1,0,2:T(8,128)S(1)}, u32[]{:S(2)}, u32[]{:S(2)}) async-start(f32[4,5,32,256]{3,1,0,2:T(8,128)} %copy.32), calls=%async_computation | async-start | bytes 2097152 | tf_op jit(solution)/shard_map/all_to_all | solution.py:163
  52.4 2.8 %copy-start.8 = (pred[4,16]{1,0:T(4,128)(4,1)S(1)}, pred[4,16]{1,0:T(4,128)(4,1)}, u32[]{:S(2)}) copy-start(pred[4,16]{1,0:T(4,128)(4,1)} %broadcast_compare_fusion) | copy-start | bytes 196
